TPU v7x, 32 devices: a whole 2x2x4 slice. The times are simulated.
32 devices in a mesh: dp: 8 (over y, x, core), mp: 4 (over z).
Axes of the slice: x: 2, y: 2, z: 4, core: 2. Of those that a mesh axis runs over, the one named last changes fastest.
Arguments:
- tokens: bfloat16 [16384, 1024], P(('dp', 'mp')), may hold values from -6 to 6
- segments: int32 [16384], P('dp'), may hold values from 0 to 68, as said below
- ln1_gain: bfloat16 [1024], replicated, may hold values from 0.5 to 1.5
- ln1_bias: bfloat16 [1024], replicated, may hold values from -1.75 to 1.75
- w_query: bfloat16 [1024, 1024], P(None, 'mp'), may hold values from -0.1875 to 0.1875
- b_query: bfloat16 [1024], P('mp'), may hold values from -3 to 3
- w_key: bfloat16 [1024, 1024], P(None, 'mp'), may hold values from -0.1875 to 0.1875
- w_value: bfloat16 [1024, 1024], P(None, 'mp'), may hold values from -0.1875 to 0.1875
- b_value: bfloat16 [1024], P('mp'), may hold values from -3 to 3
- w_out: bfloat16 [1024, 1024], P('mp'), may hold values from -0.5 to 0.5
- b_out: bfloat16 [1024], replicated, may hold values from -1.75 to 1.75
- ln2_gain: bfloat16 [1024], replicated, may hold values from 0.5 to 1.5
- ln2_bias: bfloat16 [1024], replicated, may hold values from -1.75 to 1.75
- w_up: bfloat16 [1024, 4096], P(None, 'mp'), may hold values from -0.1875 to 0.1875
- b_up: bfloat16 [4096], P('mp'), may hold values from -3 to 3
- w_down: bfloat16 [4096, 1024], P('mp'), may hold values from -0.09375 to 0.09375
- b_down: bfloat16 [1024], replicated, may hold values from -1.75 to 1.75
- cotangent: bfloat16 [16384, 1024], P(('dp', 'mp')), may hold values from -6 to 6
Outputs:
- output: bfloat16 [16384, 1024], P(('dp', 'mp'))
- grad_tokens: float32 [16384, 1024], P(('dp', 'mp'))
- grad_ln1_gain: float32 [1024], replicated
- grad_ln1_bias: float32 [1024], replicated
- grad_w_query: float32 [1024, 1024], P(None, 'mp')
- grad_b_query: float32 [1024], P('mp')
- grad_w_key: float32 [1024, 1024], P(None, 'mp')
- grad_w_value: float32 [1024, 1024], P(None, 'mp')
- grad_b_value: float32 [1024], P('mp')
- grad_w_out: float32 [1024, 1024], P('mp')
- grad_b_out: float32 [1024], replicated
- grad_ln2_gain: float32 [1024], replicated
- grad_ln2_bias: float32 [1024], replicated
- grad_w_up: float32 [1024, 4096], P(None, 'mp')
- grad_b_up: float32 [4096], P('mp')
- grad_w_down: float32 [4096, 1024], P('mp')
- grad_b_down: float32 [1024], replicated
Inputs may be any that keep to these rules, and one draw needn't show every extreme that they name: `segments`: within each group of 2048 rows the ids start at 0 and rise by one from image to image, so an image's patches are consecutive rows. Small images have 30 to 48 patches; in some groups, and always in at least one, the first image has exactly 900 patches; in at least one other group every image has exactly 30 patches; the last image of a group may have fewer patches. No image has more than 900 patches.
All inputs are finite; a program needn't handle non-finite values.
Results may differ from a plain program's by a relative error of at most 0.019.
Values may be sent and summed in bfloat16 or wider, within the bound.
A program may use at most 128 MiB of HBM per device.

v0:
```python
import jax
import jax.numpy as jnp
from jax import lax
from jax.sharding import PartitionSpec as P

HEAD_DIM = 64
epsilon = 1e-06
minus_big = -1e30


def matmul(left, right):
    return jnp.dot(left, right, preferred_element_type=jnp.float32)


def times_transposed(left, right):
    return lax.dot_general(
        left, right, (((1,), (1,)), ((), ())), preferred_element_type=jnp.float32
    )


def transposed_times(left, right):
    return lax.dot_general(
        left, right, (((0,), (0,)), ((), ())), preferred_element_type=jnp.float32
    )


def normalize(values):
    average = jnp.mean(values, axis=1, keepdims=True)
    centered = values - average
    spread = jnp.mean(centered * centered, axis=1, keepdims=True)
    inv_std = lax.rsqrt(spread + epsilon)
    return (centered * inv_std, inv_std)


def norm_back(grad_norm, x_hat, inv_std, gain_vec):
    grad_hat = grad_norm * gain_vec
    first = jnp.mean(grad_hat, axis=1, keepdims=True)
    second = jnp.mean(grad_hat * x_hat, axis=1, keepdims=True)
    grad_input = inv_std * (grad_hat - first - x_hat * second)
    return (grad_input, jnp.sum(grad_norm * x_hat, axis=0), jnp.sum(grad_norm, axis=0))


def gelu_slope(values):
    cdf_part = 0.5 * (1.0 + lax.erf(values * 0.7071067811865476))
    return cdf_part + values * jnp.exp(-0.5 * values * values) * 0.3989422804014327


def local(
    tokens,
    segments,
    ln1_gain,
    ln1_bias,
    w_query,
    b_query,
    w_key,
    w_value,
    b_value,
    w_out,
    b_out,
    ln2_gain,
    ln2_bias,
    w_up,
    b_up,
    w_down,
    b_down,
    cotangent,
):
    all_rows = segments.shape[0]
    local_width = w_query.shape[1]
    head_count = local_width // HEAD_DIM
    score_scale = HEAD_DIM ** (-0.5)
    block_rows = min(512, all_rows)
    block_count = all_rows // block_rows
    gain_one = ln1_gain.astype(jnp.float32)
    bias_one = ln1_bias.astype(jnp.float32)
    gain_two = ln2_gain.astype(jnp.float32)
    bias_two = ln2_bias.astype(jnp.float32)
    resid_in = tokens.astype(jnp.float32)
    hat_one, inv_one = normalize(resid_in)
    normed_one = (hat_one * gain_one + bias_one).astype(jnp.bfloat16)
    gathered_one = lax.all_gather(normed_one, "mp", axis=0, tiled=True)
    query = (matmul(gathered_one, w_query) + b_query.astype(jnp.float32)).astype(jnp.bfloat16)
    keys = matmul(gathered_one, w_key).astype(jnp.bfloat16)
    values = (matmul(gathered_one, w_value) + b_value.astype(jnp.float32)).astype(jnp.bfloat16)
    query_blocks = query.reshape(block_count, block_rows, head_count, HEAD_DIM)
    segment_blocks = segments.reshape(block_count, block_rows)
    keys_heads = keys.reshape(all_rows, head_count, HEAD_DIM)
    values_heads = values.reshape(all_rows, head_count, HEAD_DIM)

    def scores_of(query_block, segment_block):
        raw_scores = (
            jnp.einsum("qhd,khd->hqk", query_block, keys_heads, preferred_element_type=jnp.float32)
            * score_scale
        )
        same_image = (segment_block[:, None] == segments[None, :])[None]
        return jnp.where(same_image, raw_scores, minus_big)

    def forward_block(pieces):
        query_block, segment_block = pieces
        scores = scores_of(query_block, segment_block)
        row_max = jnp.max(scores, axis=2, keepdims=True)
        exp_scores = jnp.exp(scores - row_max)
        row_sum = jnp.sum(exp_scores, axis=2, keepdims=True)
        probabilities = (exp_scores / row_sum).astype(jnp.bfloat16)
        head_out = jnp.einsum(
            "hqk,khd->qhd", probabilities, values_heads, preferred_element_type=jnp.float32
        )
        return (head_out.astype(jnp.bfloat16), row_max[:, :, 0] + jnp.log(row_sum[:, :, 0]))

    attn_blocks, log_totals = lax.map(forward_block, (query_blocks, segment_blocks))
    attn_out = attn_blocks.reshape(all_rows, local_width)
    attn_branch = lax.psum_scatter(
        matmul(attn_out, w_out).astype(jnp.bfloat16), "mp", scatter_dimension=0, tiled=True
    ).astype(jnp.float32)
    hidden_one = resid_in + attn_branch + b_out.astype(jnp.float32)
    hat_two, inv_two = normalize(hidden_one)
    normed_two = (hat_two * gain_two + bias_two).astype(jnp.bfloat16)
    gathered_two = lax.all_gather(normed_two, "mp", axis=0, tiled=True)
    upper = matmul(gathered_two, w_up) + b_up.astype(jnp.float32)
    active = jax.nn.gelu(upper, approximate=False).astype(jnp.bfloat16)
    mlp_branch = lax.psum_scatter(
        matmul(active, w_down).astype(jnp.bfloat16), "mp", scatter_dimension=0, tiled=True
    ).astype(jnp.float32)
    output = (hidden_one + mlp_branch + b_down.astype(jnp.float32)).astype(jnp.bfloat16)
    grad_out = cotangent.astype(jnp.float32)
    grad_b_down = jnp.sum(grad_out, axis=0)
    grad_rows = lax.all_gather(cotangent, "mp", axis=0, tiled=True)
    grad_w_down = transposed_times(active, grad_rows)
    grad_active = times_transposed(grad_rows, w_down)
    grad_upper = (grad_active * gelu_slope(upper)).astype(jnp.bfloat16)
    grad_b_up = jnp.sum(grad_upper, axis=0, dtype=jnp.float32)
    grad_w_up = transposed_times(gathered_two, grad_upper)
    grad_normed_two = lax.psum_scatter(
        times_transposed(grad_upper, w_up).astype(jnp.bfloat16),
        "mp",
        scatter_dimension=0,
        tiled=True,
    ).astype(jnp.float32)
    grad_hidden, grad_ln2_gain, grad_ln2_bias = norm_back(
        grad_normed_two, hat_two, inv_two, gain_two
    )
    grad_hidden = grad_hidden + grad_out
    grad_b_out = jnp.sum(grad_hidden, axis=0)
    hidden_rows = lax.all_gather(grad_hidden.astype(jnp.bfloat16), "mp", axis=0, tiled=True)
    grad_w_out = transposed_times(attn_out, hidden_rows)
    grad_attn = times_transposed(hidden_rows, w_out).astype(jnp.bfloat16)
    grad_attn_blocks = grad_attn.reshape(block_count, block_rows, head_count, HEAD_DIM)

    def backward_block(carry, pieces):
        grad_keys_sum, grad_values_sum = carry
        query_block, segment_block, log_block, grad_block = pieces
        scores = scores_of(query_block, segment_block)
        probabilities = jnp.exp(scores - log_block[:, :, None])
        grad_probs = jnp.einsum(
            "qhd,khd->hqk", grad_block, values_heads, preferred_element_type=jnp.float32
        )
        inner = jnp.sum(probabilities * grad_probs, axis=2, keepdims=True)
        grad_scores = (probabilities * (grad_probs - inner)).astype(jnp.bfloat16)
        grad_query_block = (
            jnp.einsum("hqk,khd->qhd", grad_scores, keys_heads, preferred_element_type=jnp.float32)
            * score_scale
        )
        grad_keys_sum = (
            grad_keys_sum
            + jnp.einsum(
                "hqk,qhd->khd", grad_scores, query_block, preferred_element_type=jnp.float32
            )
            * score_scale
        )
        grad_values_sum = grad_values_sum + jnp.einsum(
            "hqk,qhd->khd",
            probabilities.astype(jnp.bfloat16),
            grad_block,
            preferred_element_type=jnp.float32,
        )
        return ((grad_keys_sum, grad_values_sum), grad_query_block.astype(jnp.bfloat16))

    zeros_heads = jnp.zeros((all_rows, head_count, HEAD_DIM), jnp.float32)
    (grad_keys_sum, grad_values_sum), grad_query_blocks = lax.scan(
        backward_block,
        (zeros_heads, zeros_heads),
        (query_blocks, segment_blocks, log_totals, grad_attn_blocks),
    )
    grad_query = grad_query_blocks.reshape(all_rows, local_width)
    grad_keys = grad_keys_sum.reshape(all_rows, local_width).astype(jnp.bfloat16)
    grad_values = grad_values_sum.reshape(all_rows, local_width).astype(jnp.bfloat16)
    grad_w_query = transposed_times(gathered_one, grad_query)
    grad_b_query = jnp.sum(grad_query, axis=0, dtype=jnp.float32)
    grad_w_key = transposed_times(gathered_one, grad_keys)
    grad_w_value = transposed_times(gathered_one, grad_values)
    grad_b_value = jnp.sum(grad_values, axis=0, dtype=jnp.float32)
    term = times_transposed(grad_query, w_query)
    term = term + times_transposed(grad_keys, w_key)
    grad_normed_one = lax.psum_scatter(
        (term + times_transposed(grad_values, w_value)).astype(jnp.bfloat16),
        "mp",
        scatter_dimension=0,
        tiled=True,
    ).astype(jnp.float32)
    grad_input, grad_ln1_gain, grad_ln1_bias = norm_back(
        grad_normed_one, hat_one, inv_one, gain_one
    )
    grad_tokens = grad_input + grad_hidden
    (
        grad_w_query,
        grad_b_query,
        grad_w_key,
        grad_w_value,
        grad_b_value,
        grad_w_out,
        grad_w_up,
        grad_b_up,
        grad_w_down,
    ) = (
        lax.psum(grad_w_query.astype(jnp.bfloat16), "dp").astype(jnp.float32),
        lax.psum(grad_b_query.astype(jnp.bfloat16), "dp").astype(jnp.float32),
        lax.psum(grad_w_key.astype(jnp.bfloat16), "dp").astype(jnp.float32),
        lax.psum(grad_w_value.astype(jnp.bfloat16), "dp").astype(jnp.float32),
        lax.psum(grad_b_value.astype(jnp.bfloat16), "dp").astype(jnp.float32),
        lax.psum(grad_w_out.astype(jnp.bfloat16), "dp").astype(jnp.float32),
        lax.psum(grad_w_up.astype(jnp.bfloat16), "dp").astype(jnp.float32),
        lax.psum(grad_b_up.astype(jnp.bfloat16), "dp").astype(jnp.float32),
        lax.psum(grad_w_down.astype(jnp.bfloat16), "dp").astype(jnp.float32),
    )
    grad_ln1_gain, grad_ln1_bias, grad_b_out, grad_ln2_gain, grad_ln2_bias, grad_b_down = lax.psum(
        (grad_ln1_gain, grad_ln1_bias, grad_b_out, grad_ln2_gain, grad_ln2_bias, grad_b_down),
        ("dp", "mp"),
    )
    return (
        output,
        grad_tokens,
        grad_ln1_gain,
        grad_ln1_bias,
        grad_w_query,
        grad_b_query,
        grad_w_key,
        grad_w_value,
        grad_b_value,
        grad_w_out,
        grad_b_out,
        grad_ln2_gain,
        grad_ln2_bias,
        grad_w_up,
        grad_b_up,
        grad_w_down,
        grad_b_down,
    )


def solution(mesh):
    in_specs = (
        P(("dp", "mp"), None),
        P("dp"),
        P(),
        P(),
        P(None, "mp"),
        P("mp"),
        P(None, "mp"),
        P(None, "mp"),
        P("mp"),
        P("mp", None),
        P(),
        P(),
        P(),
        P(None, "mp"),
        P("mp"),
        P("mp", None),
        P(),
        P(("dp", "mp"), None),
    )
    out_specs = (
        P(("dp", "mp"), None),
        P(("dp", "mp"), None),
        P(),
        P(),
        P(None, "mp"),
        P("mp"),
        P(None, "mp"),
        P(None, "mp"),
        P("mp"),
        P("mp", None),
        P(),
        P(),
        P(),
        P(None, "mp"),
        P("mp"),
        P("mp", None),
        P(),
    )
    return jax.shard_map(local, mesh=mesh, in_specs=in_specs, out_specs=out_specs, check_vma=False)
```

profile of v0, /device:TPU:0, one launch (start us, length us, event | category | flops | bytes accessed | tf_op | source)
XLA Modules:
  0.0 1142.3 jit_solution(16438787603620042261)
XLA Ops:
  14.7 83.5 %all-gather.5.cloned.1.call-done = bf16[2048,1024]{1,0:T(8,128)(2,1)} async-done(((bf16[512,1024]{1,0:T(8,128)(2,1)}), bf16[2048,1024]{1,0:T(8,128)(2,1)}) %all-gather.5.cloned.1.call-update) | async-done | bytes 4194320 | tf_op jit(solution)/shard_map/all_gather | solution.py:81
  114.7 64.4 %while.27 = (s32[]{:T(128)}, bf16[4,512,4,64]{1,3,2,0:T(8,128)(2,1)}, f32[4,4,512]{2,1,0:T(4,128)}, s32[4,512]{1,0:T(4,128)S(1)}, s32[2048]{0:T(1024)S(1)}, /*in...) while((s32[]{:T(128)}, ...), condition=%wide.region_5.6_spmd, body=%wide.region_2.5_spmd.sunk | while | flops 1125251072 | bytes 57227380 | solution.py:110
  186.8 74.8 %reduce-scatter.5.cloned.1.call-done = bf16[512,1024]{1,0:T(8,128)(2,1)} async-done(((bf16[2048,1024]{1,0:T(8,128)(2,1)}), bf16[512,1024]{1,0:T(8,128)(2,1)}) %reduce-scatter.5.cloned.1.call-update) | async-done | bytes 1048592 | tf_op jit(solution)/shard_map/reduce_scatter | solution.py:112
  267.4 80.8 %all-gather.7.cloned.1.call-done = bf16[2048,1024]{1,0:T(8,128)(2,1)} async-done(((bf16[512,1024]{1,0:T(8,128)(2,1)}), bf16[2048,1024]{1,0:T(8,128)(2,1)}) %all-gather.7.cloned.1.call-update) | async-done | bytes 4194320 | tf_op jit(solution)/shard_map/all_gather | solution.py:118
  348.2 25.0 %fusion.45 = (bf16[2048,1024]{1,0:T(8,128)(2,1)}, f32[2048,1024]{1,0:T(8,128)}) fusion(f32[1024]{0:T(1024)S(1)} %convert_element_type.187, bf16[2048,1024]{1,0:T(8,128)(2,1)} %all-gather.7.cloned.1.call-done, bf16[1024,1024]{1,0:T(8,128)(2,1)S(1)} %copy-done), kind=kOutput, calls=%fused_computation.56 | convolution fusion | flops 4433379328 | bytes 18878464 | tf_op jit(solution)/shard_map/dot_general | solution.py:12
  373.2 55.6 %all-gather.9.cloned.1.call-done = bf16[2048,1024]{1,0:T(8,128)(2,1)} async-done(((bf16[512,1024]{1,0:T(8,128)(2,1)}), bf16[2048,1024]{1,0:T(8,128)(2,1)}) %all-gather.9.cloned.1.call-update) | async-done | bytes 4194320 | tf_op jit(solution)/shard_map/all_gather | solution.py:127
  428.9 11.9 %fusion.87 = (bf16[1024]{0:T(1024)(128)(2,1)}, bf16[2048,1024]{1,0:T(8,128)(2,1)S(1)}) fusion(f32[2048,1024]{1,0:T(8,128)} %get-tuple-element.270, f32[1024]{0:T(1024)S(1)} %convert_element_type.187, bf16[2048,1024]{1,0:T(8,128)(2,1)} %all-gather.9.cloned.1.call-done, bf16[1024,1024]{1,0:T(8,128)(2,1)} %param.37), kind=kOutput, calls=%fused_computation.143 | convolution fusion | flops 4320132096 | bytes 18880512 | tf_op jit(solution)/shard_map/dot_general | solution.py:16
  459.5 64.9 %reduce-scatter.9.cloned.1.call-done = bf16[512,1024]{1,0:T(8,128)(2,1)} async-done(((bf16[2048,1024]{1,0:T(8,128)(2,1)}), bf16[512,1024]{1,0:T(8,128)(2,1)}) %reduce-scatter.9.cloned.1.call-update) | async-done | bytes 1048592 | tf_op jit(solution)/shard_map/reduce_scatter | solution.py:133
  527.4 76.5 %reduce-scatter.7.cloned.1.call-done = bf16[512,1024]{1,0:T(8,128)(2,1)} async-done(((bf16[2048,1024]{1,0:T(8,128)(2,1)}), bf16[512,1024]{1,0:T(8,128)(2,1)}) %reduce-scatter.7.cloned.1.call-update) | async-done | bytes 1048592 | tf_op jit(solution)/shard_map/reduce_scatter | solution.py:121
  610.6 9.5 convolution_convert_fusion.5
  625.9 66.0 %all-gather.11.cloned.1.call-done = bf16[2048,1024]{1,0:T(8,128)(2,1)} async-done(((bf16[512,1024]{1,0:T(8,128)(2,1)}), bf16[2048,1024]{1,0:T(8,128)(2,1)}) %all-gather.11.cloned.1.call-update) | async-done | bytes 4194320 | tf_op jit(solution)/shard_map/all_gather | solution.py:144
  699.7 191.3 %while.28 = (s32[]{:T(128)}, f32[2048,4,64]{0,2,1:T(8,128)}, f32[2048,4,64]{0,2,1:T(8,128)}, bf16[4,512,4,64]{1,3,2,0:T(8,128)(2,1)}, bf16[4,512,4,64]{1,3,2,0:T...) while((s32[]{:T(128)}, f32[2048,4,64]{0,2,1:T(8,128)}, ...), condition=%wide.region_15.16_spmd.clone, body=%wide.region_13.15_spmd.clone.sunk | while | flops 2751199232 | bytes 176625968 | solution.py:179
  713.5 11.3 multiply_reduce_fusion.3
  724.8 10.8 multiply_convert_fusion.2
  760.7 11.3 multiply_reduce_fusion.3
  772.0 10.8 multiply_convert_fusion.2
  808.7 11.3 multiply_reduce_fusion.3
  820.0 10.8 multiply_convert_fusion.2
  856.6 11.3 multiply_reduce_fusion.3
  867.9 10.8 multiply_convert_fusion.2
  914.5 14.5 %all-reduce.1 = (bf16[256]{0:T(256)(128)(2,1)S(1)}, bf16[256]{0:T(256)(128)(2,1)S(1)}, bf16[1024]{0:T(1024)(128)(2,1)S(1)}) all-reduce(bf16[256]{0:T(256)(128)(2,1)S(1)} %reduce_sum.195, bf16[256]{0:T(256)(128)(2,1)S(1)} %reduce_sum.197, bf16[1024]{0:T(1024)(128)(2,1)S(1)} %copy-done.41), channel_id=1, replica_groups=mesh['dp'=8,'mp'=4] {'dp'}, use_global_device_ids=true, to_apply=%region_25.26 | all-reduce | flops 1536 | bytes 6144 | tf_op jit(solution)/shard_map/psum | solution.py:216
  930.7 78.0 %all-reduce.5.cloned.1.call-done = (bf16[1024,256]{1,0:T(8,128)(2,1)}, bf16[1024,256]{1,0:T(8,128)(2,1)}, bf16[1024,256]{1,0:T(8,128)(2,1)}, bf16[256,1024]{1,0:...) async-done(((bf16[1024,256]{1,0:T(8,128)(2,1)}, bf16[1024,256]{1,0:T(8,128)(2,1)}, bf16[1024,256]{1,0:T(8,128)(2,1)}, bf16[256,1024]{1,0:T(8,128)(2,1)}, ...) | async-done | bytes 6291472 | tf_op jit(solution)/shard_map/psum | solution.py:215
  1021.3 66.7 %reduce-scatter.11.cloned.1.call-done = bf16[512,1024]{1,0:T(8,128)(2,1)} async-done(((bf16[2048,1024]{1,0:T(8,128)(2,1)}), bf16[512,1024]{1,0:T(8,128)(2,1)}) %reduce-scatter.11.cloned.1.call-update) | async-done | bytes 1048592 | tf_op jit(solution)/shard_map/reduce_scatter | solution.py:194
  1090.3 41.4 %all-reduce = (f32[1024]{0:T(1024)}, f32[1024]{0:T(1024)}, f32[1024]{0:T(1024)}, f32[1024]{0:T(1024)}, f32[1024]{0:T(1024)}, /*index=5*/f32[1024]{0:T(1024)}) all-reduce(f32[1024]{0:T(1024)S(1)} %get-tuple-element.200, f32[1024]{0:T(1024)S(1)} %get-tuple-element.205, ...), channel_id=1, replica_groups=mesh['dp'=8,'mp'=4] {'dp','mp'}, use_global_device_ids=true, to_apply=%region_20.21 | all-reduce | flops 6144 | bytes 49152 | tf_op jit(solution)/shard_map/psum | solution.py:225
  (272 shorter events, 289.3 us)
Async XLA Ops:
  7.2 341.0 %copy-start = (bf16[1024,1024]{1,0:T(8,128)(2,1)S(1)}, bf16[1024,1024]{1,0:T(8,128)(2,1)}, u32[]{:S(2)}) copy-start(bf16[1024,1024]{1,0:T(8,128)(2,1)} %param.35) | copy-start | bytes 6291460
  7.2 91.0 %all-gather.5.cloned.1.call-start = ((), (), s32[]{:S(2)}) async-start(), calls=%async_computation.4 | async-start | bytes 5242880 | tf_op jit(solution)/shard_map/all_gather | solution.py:81
  14.6 247.0 %reduce-scatter.5.cloned.1.call-start = ((), (), s32[]{:S(2)}) async-start(), calls=%async_computation.5 | async-start | bytes 5242880 | tf_op jit(solution)/shard_map/reduce_scatter | solution.py:112
  186.1 75.5 %copy-start.3 = (bf16[512,1024]{1,0:T(8,128)(2,1)S(1)}, bf16[512,1024]{1,0:T(8,128)(2,1)}, u32[]{:S(2)}) copy-start(bf16[512,1024]{1,0:T(8,128)(2,1)} %param.22) | copy-start | bytes 3145732
  186.2 162.0 %all-gather.7.cloned.1.call-start = ((), (), s32[]{:S(2)}) async-start(), calls=%async_computation.6 | async-start | bytes 5242880 | tf_op jit(solution)/shard_map/all_gather | solution.py:118
  266.8 162.1 %all-gather.9.cloned.1.call-start = ((), (), s32[]{:S(2)}) async-start(), calls=%async_computation.8 | async-start | bytes 5242880 | tf_op jit(solution)/shard_map/all_gather | solution.py:127
  267.4 257.0 %reduce-scatter.9.cloned.1.call-start = ((), (), s32[]{:S(2)}) async-start(), calls=%async_computation.9 | async-start | bytes 5242880 | tf_op jit(solution)/shard_map/reduce_scatter | solution.py:133
  449.0 154.9 %reduce-scatter.7.cloned.1.call-start = ((), (), s32[]{:S(2)}) async-start(), calls=%async_computation.7 | async-start | bytes 5242880 | tf_op jit(solution)/shard_map/reduce_scatter | solution.py:121
  458.9 65.5 %copy-start.7 = (bf16[512,1024]{1,0:T(8,128)(2,1)S(1)}, bf16[512,1024]{1,0:T(8,128)(2,1)}, u32[]{:S(2)}) copy-start(bf16[512,1024]{1,0:T(8,128)(2,1)} %reduce-scatter.5.cloned.1.call-done) | copy-start | bytes 3145732
  458.9 145.0 %copy-start.12 = (bf16[512,1024]{1,0:T(8,128)(2,1)S(1)}, bf16[512,1024]{1,0:T(8,128)(2,1)}, u32[]{:S(2)}) copy-start(bf16[512,1024]{1,0:T(8,128)(2,1)} %param.39) | copy-start | bytes 3145732
  458.9 233.1 %all-gather.11.cloned.1.call-start = ((), (), s32[]{:S(2)}) async-start(), calls=%async_computation.10 | async-start | bytes 5242880 | tf_op jit(solution)/shard_map/all_gather | solution.py:144
  610.6 398.2 %all-reduce.5.cloned.1.call-start = ((), (), s32[]{:S(2)}) async-start(), calls=%async_computation.12 | async-start | bytes 12582912 | tf_op jit(solution)/shard_map/psum | solution.py:215
  610.6 9.5 copy-start.45
  620.2 71.8 %copy-start.19 = (bf16[256,1024]{1,0:T(8,128)(2,1)S(1)}, bf16[256,1024]{1,0:T(8,128)(2,1)}, u32[]{:S(2)}) copy-start(bf16[256,1024]{1,0:T(8,128)(2,1)} %param.31) | copy-start | bytes 1572868
  905.6 182.4 %reduce-scatter.11.cloned.1.call-start = ((), (), s32[]{:S(2)}) async-start(), calls=%async_computation.11 | async-start | bytes 5242880 | tf_op jit(solution)/shard_map/reduce_scatter | solution.py:194
  1018.7 69.3 %copy-start.4 = (bf16[512,1024]{1,0:T(8,128)(2,1)S(1)}, bf16[512,1024]{1,0:T(8,128)(2,1)}, u32[]{:S(2)}) copy-start(bf16[512,1024]{1,0:T(8,128)(2,1)} %param.22) | copy-start | bytes 3145732
  1018.7 69.3 %copy-start.27 = (f32[1024]{0:T(1024)S(1)}, f32[1024]{0:T(1024)}, u32[]{:S(2)}) copy-start(f32[1024]{0:T(1024)} %copy-done.26) | copy-start | bytes 12292
  1018.7 69.3 %copy-start.29 = (f32[512]{0:T(512)S(1)}, f32[512]{0:T(512)}, u32[]{:S(2)}) copy-start(f32[512]{0:T(512)} %copy-done.28) | copy-start | bytes 6148
  1018.7 69.3 %copy-start.31 = (f32[512]{0:T(512)S(1)}, f32[512]{0:T(512)}, u32[]{:S(2)}) copy-start(f32[512]{0:T(512)} %copy-done.30) | copy-start | bytes 6148
  1018.7 71.5 %copy-start.32 = (f32[1024]{0:T(1024)S(1)}, f32[1024]{0:T(1024)}, u32[]{:S(2)}) copy-start(f32[1024]{0:T(1024)} %get-tuple-element.198) | copy-start | bytes 12292
  1018.7 71.5 %copy-start.33 = (f32[1024]{0:T(1024)S(1)}, f32[1024]{0:T(1024)}, u32[]{:S(2)}) copy-start(f32[1024]{0:T(1024)} %get-tuple-element.204) | copy-start | bytes 12292
  1018.8 71.5 %copy-start.34 = (f32[1024]{0:T(1024)S(1)}, f32[1024]{0:T(1024)}, u32[]{:S(2)}) copy-start(f32[1024]{0:T(1024)} %get-tuple-element.261) | copy-start | bytes 12292
  1018.8 71.5 %copy-start.35 = (f32[1024]{0:T(1024)S(1)}, f32[1024]{0:T(1024)}, u32[]{:S(2)}) copy-start(f32[1024]{0:T(1024)} %get-tuple-element.268) | copy-start | bytes 12292
  1018.8 116.8 %copy-start.1 = (bf16[1024,1024]{1,0:T(8,128)(2,1)S(1)}, bf16[1024,1024]{1,0:T(8,128)(2,1)}, u32[]{:S(2)}) copy-start(bf16[1024,1024]{1,0:T(8,128)(2,1)} %param.35) | copy-start | bytes 6291460
  (51 other events, 181.5 us)
Sparse Core Ops, SparseCore 0:
  14.7 83.4 all-gather.4
  186.3 75.2 reduce-scatter.4
  266.9 81.2 all-gather.6
  349.6 79.2 all-gather.8
  449.1 75.2 reduce-scatter.8
  526.5 77.2 reduce-scatter.6
  610.7 81.2 all-gather.10
  905.7 102.9 all-reduce.4
  1011.0 76.9 reduce-scatter.10
where the time goes:
time: 1150 us; the launch traced here: 1140 us
  waiting for transfers between devices  647 us (56%)
  matrix products  277 us (24%)
  other arithmetic  116 us (10%)
  blocking collectives  55.9 us (5%)
  local copies, waits for them, and re-layouts  29.5 us (3%)
  between operations  14.6 us (1%)
    all_gather x1, waiting for transfers between devices, local(): gathered_one = lax.all_gather(normed_one, 'mp', axis=0, tiled=True)  83.5 us
    all_gather x1, waiting for transfers between devices, local(): gathered_two = lax.all_gather(normed_two, 'mp', axis=0, tiled=True)  80.8 us
    psum x1, waiting for transfers between devices, local(): lax.psum(grad_w_query.astype(jnp.bfloat16), 'dp').astype(jnp.float32)  78 us
    reduce_scatter x1, waiting for transfers between devices, local(): lax.psum_scatter(matmul(active, w_down).astype(jnp.bfloat16), 'mp', scatt...  76.5 us
    reduce_scatter x1, waiting for transfers between devices, local(): lax.psum_scatter(matmul(attn_out, w_out).astype(jnp.bfloat16), 'mp', scat...  74.8 us
    reduce_scatter x1, waiting for transfers between devices, local(): lax.psum_scatter((term + times_transposed(grad_values, w_value)).astype(j...  66.7 us
    all_gather x1, waiting for transfers between devices, local(): lax.all_gather(grad_hidden.astype(jnp.bfloat16), 'mp', axis=0, tiled=True)  66 us
    reduce_scatter x1, waiting for transfers between devices, local(): lax.psum_scatter(times_transposed(grad_upper, w_up).astype(jnp.bfloat16),...  64.9 us
  transfers between devices with their start and end apart: 9, of which 9 were waited for; matrix products, arithmetic and copies ran while one was open for 6% of the time, Pallas kernels for 0%

commit v1 on v0

--- a/solution.py
+++ b/solution.py
@@ -141,7 +141,16 @@
     )
     grad_hidden = grad_hidden + grad_out
     grad_b_out = jnp.sum(grad_hidden, axis=0)
-    hidden_rows = lax.all_gather(grad_hidden.astype(jnp.bfloat16), "mp", axis=0, tiled=True)
+    value = grad_hidden.astype(jnp.bfloat16)
+    ways, here = (lax.axis_size("mp"), lax.axis_index("mp"))
+    grown, reach = (value, 1)
+    while reach < ways:
+        theirs = lax.ppermute(grown, "mp", [(d, d ^ reach) for d in range(ways)])
+        mine_first = jnp.concatenate([grown, theirs], axis=0)
+        theirs_first = jnp.concatenate([theirs, grown], axis=0)
+        grown = jnp.where(here & reach == 0, mine_first, theirs_first)
+        reach = 2 * reach
+    hidden_rows = grown
     grad_w_out = transposed_times(attn_out, hidden_rows)
     grad_attn = times_transposed(hidden_rows, w_out).astype(jnp.bfloat16)
     grad_attn_blocks = grad_attn.reshape(block_count, block_rows, head_count, HEAD_DIM)

time: 1150 us -> 1190 us (1.035)
  waiting for transfers between devices: 647 us -> 681 us
    ppermute x0 -> x2, waiting for transfers between devices: none -> 98.9 us  [local(): theirs = lax.ppermute(grown, 'mp', [(d, d ^ reach) for d in range(ways)])]
    all_gather x1 -> x0, waiting for transfers between devices: 66 us -> none  [local(): lax.all_gather(grad_hidden.astype(jnp.bfloat16), 'mp', axis=0, tiled=True)]
  transfers between devices with their start and end apart: 9 -> 10, of which waited for: 9 -> 10; matrix products, arithmetic and copies ran while one was open for 6% -> 6% of each run, Pallas kernels for 0% -> 0%
where the time goes in v1:
time: 1190 us; the launch traced here: 1180 us
  waiting for transfers between devices  681 us (57%)
  matrix products  277 us (23%)
  other arithmetic  116 us (10%)
  blocking collectives  56 us (5%)
  local copies, waits for them, and re-layouts  30.8 us (3%)
  between operations  15.1 us (1%)
    ppermute x2, waiting for transfers between devices, local(): theirs = lax.ppermute(grown, 'mp', [(d, d ^ reach) for d in range(ways)])  98.9 us
    all_gather x1, waiting for transfers between devices, local(): gathered_one = lax.all_gather(normed_one, 'mp', axis=0, tiled=True)  83.5 us
    all_gather x1, waiting for transfers between devices, local(): gathered_two = lax.all_gather(normed_two, 'mp', axis=0, tiled=True)  80.7 us
    psum x1, waiting for transfers between devices, local(): lax.psum(grad_w_query.astype(jnp.bfloat16), 'dp').astype(jnp.float32)  79.2 us
    reduce_scatter x1, waiting for transfers between devices, local(): lax.psum_scatter(matmul(active, w_down).astype(jnp.bfloat16), 'mp', scatt...  76.5 us
    reduce_scatter x1, waiting for transfers between devices, local(): lax.psum_scatter(matmul(attn_out, w_out).astype(jnp.bfloat16), 'mp', scat...  74.8 us
    reduce_scatter x1, waiting for transfers between devices, local(): lax.psum_scatter((term + times_transposed(grad_values, w_value)).astype(j...  66.7 us
    reduce_scatter x1, waiting for transfers between devices, local(): lax.psum_scatter(times_transposed(grad_upper, w_up).astype(jnp.bfloat16),...  64.9 us
  transfers between devices with their start and end apart: 10, of which 10 were waited for; matrix products, arithmetic and copies ran while one was open for 6% of the time, Pallas kernels for 0%

profile of v1, /device:TPU:0, one launch (start us, length us, event | category | flops | bytes accessed | tf_op | source)
XLA Modules:
  0.0 1182.8 jit_solution(8734353460055208783)
XLA Ops:
  14.7 83.5 %all-gather.4.cloned.1.call-done = bf16[2048,1024]{1,0:T(8,128)(2,1)} async-done(((bf16[512,1024]{1,0:T(8,128)(2,1)}), bf16[2048,1024]{1,0:T(8,128)(2,1)}) %all-gather.4.cloned.1.call-update) | async-done | bytes 4194320 | tf_op jit(solution)/shard_map/all_gather | solution.py:81
  114.7 64.4 %while.27 = (s32[]{:T(128)}, bf16[4,512,4,64]{1,3,2,0:T(8,128)(2,1)}, f32[4,4,512]{2,1,0:T(4,128)}, s32[4,512]{1,0:T(4,128)S(1)}, s32[2048]{0:T(1024)S(1)}, /*in...) while((s32[]{:T(128)}, ...), condition=%wide.region_5.6_spmd, body=%wide.region_2.5_spmd.sunk | while | flops 1125251072 | bytes 57227380 | solution.py:110
  186.9 74.8 %reduce-scatter.5.cloned.1.call-done = bf16[512,1024]{1,0:T(8,128)(2,1)} async-done(((bf16[2048,1024]{1,0:T(8,128)(2,1)}), bf16[512,1024]{1,0:T(8,128)(2,1)}) %reduce-scatter.5.cloned.1.call-update) | async-done | bytes 1048592 | tf_op jit(solution)/shard_map/reduce_scatter | solution.py:112
  267.4 80.7 %all-gather.6.cloned.1.call-done = bf16[2048,1024]{1,0:T(8,128)(2,1)} async-done(((bf16[512,1024]{1,0:T(8,128)(2,1)}), bf16[2048,1024]{1,0:T(8,128)(2,1)}) %all-gather.6.cloned.1.call-update) | async-done | bytes 4194320 | tf_op jit(solution)/shard_map/all_gather | solution.py:118
  348.2 25.0 %fusion.45 = (bf16[2048,1024]{1,0:T(8,128)(2,1)}, f32[2048,1024]{1,0:T(8,128)}) fusion(f32[1024]{0:T(1024)S(1)} %convert_element_type.187, bf16[2048,1024]{1,0:T(8,128)(2,1)} %all-gather.6.cloned.1.call-done, bf16[1024,1024]{1,0:T(8,128)(2,1)S(1)} %copy-done), kind=kOutput, calls=%fused_computation.56 | convolution fusion | flops 4433379328 | bytes 18878464 | tf_op jit(solution)/shard_map/dot_general | solution.py:12
  373.2 55.6 %all-gather.8.cloned.1.call-done = bf16[2048,1024]{1,0:T(8,128)(2,1)} async-done(((bf16[512,1024]{1,0:T(8,128)(2,1)}), bf16[2048,1024]{1,0:T(8,128)(2,1)}) %all-gather.8.cloned.1.call-update) | async-done | bytes 4194320 | tf_op jit(solution)/shard_map/all_gather | solution.py:127
  428.8 11.9 %fusion.89 = (bf16[1024]{0:T(1024)(128)(2,1)}, bf16[2048,1024]{1,0:T(8,128)(2,1)S(1)}) fusion(f32[2048,1024]{1,0:T(8,128)} %get-tuple-element.270, f32[1024]{0:T(1024)S(1)} %convert_element_type.187, bf16[2048,1024]{1,0:T(8,128)(2,1)} %all-gather.8.cloned.1.call-done, bf16[1024,1024]{1,0:T(8,128)(2,1)} %param.37), kind=kOutput, calls=%fused_computation.147 | convolution fusion | flops 4320132096 | bytes 18880512 | tf_op jit(solution)/shard_map/dot_general | solution.py:16
  459.5 64.9 %reduce-scatter.9.cloned.1.call-done = bf16[512,1024]{1,0:T(8,128)(2,1)} async-done(((bf16[2048,1024]{1,0:T(8,128)(2,1)}), bf16[512,1024]{1,0:T(8,128)(2,1)}) %reduce-scatter.9.cloned.1.call-update) | async-done | bytes 1048592 | tf_op jit(solution)/shard_map/reduce_scatter | solution.py:133
  527.4 76.5 %reduce-scatter.7.cloned.1.call-done = bf16[512,1024]{1,0:T(8,128)(2,1)} async-done(((bf16[2048,1024]{1,0:T(8,128)(2,1)}), bf16[512,1024]{1,0:T(8,128)(2,1)}) %reduce-scatter.7.cloned.1.call-update) | async-done | bytes 1048592 | tf_op jit(solution)/shard_map/reduce_scatter | solution.py:121
  611.1 23.1 %collective-permute-done = bf16[512,1024]{1,0:T(8,128)(2,1)S(1)} collective-permute-done((bf16[512,1024]{1,0:T(8,128)(2,1)S(1)}, bf16[512,1024]{1,0:T(8,128)(2,1)S(1)}, u32[]{:S(2)}, u32[]{:S(2)}) %collective-permute-start) | collective-permute-done | bytes 1048608 | tf_op jit(solution)/shard_map/ppermute | solution.py:148
  652.4 75.8 %collective-permute-done.1 = bf16[1024,1024]{1,0:T(8,128)(2,1)S(1)} collective-permute-done((bf16[1024,1024]{1,0:T(8,128)(2,1)S(1)}, bf16[1024,1024]{1,0:T(8,128)(2,1)S(1)}, u32[]{:S(2)}, u32[]{:S(2)}) %collective-permute-start.1) | collective-permute-done | bytes 2097184 | tf_op jit(solution)/shard_map/ppermute | solution.py:148
  738.2 191.1 %while.28 = (s32[]{:T(128)}, f32[2048,4,64]{0,2,1:T(8,128)}, f32[2048,4,64]{0,2,1:T(8,128)}, bf16[4,512,4,64]{1,3,2,0:T(8,128)(2,1)}, bf16[4,512,4,64]{1,3,2,0:T...) while((s32[]{:T(128)}, f32[2048,4,64]{0,2,1:T(8,128)}, ...), condition=%wide.region_15.16_spmd.clone, body=%wide.region_13.15_spmd.clone.sunk | while | flops 2751199232 | bytes 176625968 | solution.py:188
  751.9 11.3 multiply_reduce_fusion.3
  763.3 10.9 multiply_convert_fusion.2
  799.2 11.3 multiply_reduce_fusion.3
  810.5 10.9 multiply_convert_fusion.2
  847.1 11.3 multiply_reduce_fusion.3
  858.4 10.9 multiply_convert_fusion.2
  895.1 11.3 multiply_reduce_fusion.3
  906.4 10.9 multiply_convert_fusion.2
  953.1 14.6 %all-reduce.1 = (bf16[256]{0:T(256)(128)(2,1)S(1)}, bf16[256]{0:T(256)(128)(2,1)S(1)}, bf16[1024]{0:T(1024)(128)(2,1)S(1)}) all-reduce(bf16[256]{0:T(256)(128)(2,1)S(1)} %reduce_sum.195, bf16[256]{0:T(256)(128)(2,1)S(1)} %reduce_sum.197, bf16[1024]{0:T(1024)(128)(2,1)S(1)} %copy-done.43), channel_id=1, replica_groups=mesh['dp'=8,'mp'=4] {'dp'}, use_global_device_ids=true, to_apply=%region_25.26 | all-reduce | flops 1536 | bytes 6144 | tf_op jit(solution)/shard_map/psum | solution.py:225
  969.4 79.2 %all-reduce.5.cloned.1.call-done = (bf16[1024,256]{1,0:T(8,128)(2,1)}, bf16[1024,256]{1,0:T(8,128)(2,1)}, bf16[1024,256]{1,0:T(8,128)(2,1)}, bf16[256,1024]{1,0:...) async-done(((bf16[1024,256]{1,0:T(8,128)(2,1)}, bf16[1024,256]{1,0:T(8,128)(2,1)}, bf16[1024,256]{1,0:T(8,128)(2,1)}, bf16[256,1024]{1,0:T(8,128)(2,1)}, ...) | async-done | bytes 6291472 | tf_op jit(solution)/shard_map/psum | solution.py:224
  1061.2 66.7 %reduce-scatter.11.cloned.1.call-done = bf16[512,1024]{1,0:T(8,128)(2,1)} async-done(((bf16[2048,1024]{1,0:T(8,128)(2,1)}), bf16[512,1024]{1,0:T(8,128)(2,1)}) %reduce-scatter.11.cloned.1.call-update) | async-done | bytes 1048592 | tf_op jit(solution)/shard_map/reduce_scatter | solution.py:203
  1130.2 41.4 %all-reduce = (f32[1024]{0:T(1024)}, f32[1024]{0:T(1024)}, f32[1024]{0:T(1024)}, f32[1024]{0:T(1024)}, f32[1024]{0:T(1024)}, /*index=5*/f32[1024]{0:T(1024)}) all-reduce(f32[1024]{0:T(1024)S(1)} %get-tuple-element.200, f32[1024]{0:T(1024)S(1)} %get-tuple-element.205, ...), channel_id=1, replica_groups=mesh['dp'=8,'mp'=4] {'dp','mp'}, use_global_device_ids=true, to_apply=%region_20.21 | all-reduce | flops 6144 | bytes 49152 | tf_op jit(solution)/shard_map/psum | solution.py:234
  (282 shorter events, 304.7 us)
Async XLA Ops:
  7.2 341.0 %copy-start = (bf16[1024,1024]{1,0:T(8,128)(2,1)S(1)}, bf16[1024,1024]{1,0:T(8,128)(2,1)}, u32[]{:S(2)}) copy-start(bf16[1024,1024]{1,0:T(8,128)(2,1)} %param.35) | copy-start | bytes 6291460
  7.2 91.0 %all-gather.4.cloned.1.call-start = ((), (), s32[]{:S(2)}) async-start(), calls=%async_computation.4 | async-start | bytes 5242880 | tf_op jit(solution)/shard_map/all_gather | solution.py:81
  14.6 247.0 %reduce-scatter.5.cloned.1.call-start = ((), (), s32[]{:S(2)}) async-start(), calls=%async_computation.5 | async-start | bytes 5242880 | tf_op jit(solution)/shard_map/reduce_scatter | solution.py:112
  186.1 75.5 %copy-start.3 = (bf16[512,1024]{1,0:T(8,128)(2,1)S(1)}, bf16[512,1024]{1,0:T(8,128)(2,1)}, u32[]{:S(2)}) copy-start(bf16[512,1024]{1,0:T(8,128)(2,1)} %param.22) | copy-start | bytes 3145732
  186.2 162.0 %all-gather.6.cloned.1.call-start = ((), (), s32[]{:S(2)}) async-start(), calls=%async_computation.6 | async-start | bytes 5242880 | tf_op jit(solution)/shard_map/all_gather | solution.py:118
  266.8 162.1 %all-gather.8.cloned.1.call-start = ((), (), s32[]{:S(2)}) async-start(), calls=%async_computation.8 | async-start | bytes 5242880 | tf_op jit(solution)/shard_map/all_gather | solution.py:127
  267.4 257.1 %reduce-scatter.9.cloned.1.call-start = ((), (), s32[]{:S(2)}) async-start(), calls=%async_computation.9 | async-start | bytes 5242880 | tf_op jit(solution)/shard_map/reduce_scatter | solution.py:133
  449.0 154.9 %reduce-scatter.7.cloned.1.call-start = ((), (), s32[]{:S(2)}) async-start(), calls=%async_computation.7 | async-start | bytes 5242880 | tf_op jit(solution)/shard_map/reduce_scatter | solution.py:121
  458.9 145.0 %copy-start.12 = (bf16[512,1024]{1,0:T(8,128)(2,1)S(1)}, bf16[512,1024]{1,0:T(8,128)(2,1)}, u32[]{:S(2)}) copy-start(bf16[512,1024]{1,0:T(8,128)(2,1)} %param.39) | copy-start | bytes 3145732
  458.9 589.8 %all-reduce.5.cloned.1.call-start = ((), (), s32[]{:S(2)}) async-start(), calls=%async_computation.11 | async-start | bytes 12582912 | tf_op jit(solution)/shard_map/psum | solution.py:224
  609.6 24.6 %collective-permute-start = (bf16[512,1024]{1,0:T(8,128)(2,1)S(1)}, bf16[512,1024]{1,0:T(8,128)(2,1)S(1)}, u32[]{:S(2)}, u32[]{:S(2)}) collective-permute-start(bf16[512,1024]{1,0:T(8,128)(2,1)S(1)} %convert_element_type.197), channel_id=1, source_target_pairs={{0,1},{1,0},{2,3},{3,2},{4,5},{5,4},{6,7},{7,6},{8,9},{9,8},{10,11... | collective-permute-start | bytes 3145736 | tf_op jit(solution)/shard_map/ppermute | solution.py:148
  635.2 93.0 %copy-start.15 = (bf16[1024,1024]{1,0:T(8,128)(2,1)}, bf16[1024,1024]{1,0:T(8,128)(2,1)S(1)}, u32[]{:S(2)}) copy-start(bf16[1024,1024]{1,0:T(8,128)(2,1)S(1)} %maximum_select_fusion.1) | copy-start | bytes 6291460
  635.2 92.9 %collective-permute-start.1 = (bf16[1024,1024]{1,0:T(8,128)(2,1)S(1)}, bf16[1024,1024]{1,0:T(8,128)(2,1)S(1)}, u32[]{:S(2)}, u32[]{:S(2)}) collective-permute-start(bf16[1024,1024]{1,0:T(8,128)(2,1)S(1)} %maximum_select_fusion.1), channel_id=1, source_target_pairs={{0,2},{1,3},{2,0},{3,1},{4,6},{5,7},{6,4},{7,5},{8,10},{9,11},{10,... | collective-permute-start | bytes 6291464 | tf_op jit(solution)/shard_map/ppermute | solution.py:148
  646.5 82.9 %copy-start.21 = (bf16[256,1024]{1,0:T(8,128)(2,1)S(1)}, bf16[256,1024]{1,0:T(8,128)(2,1)}, u32[]{:S(2)}) copy-start(bf16[256,1024]{1,0:T(8,128)(2,1)} %param.31) | copy-start | bytes 1572868
  944.0 183.9 %reduce-scatter.11.cloned.1.call-start = ((), (), s32[]{:S(2)}) async-start(), calls=%async_computation.10 | async-start | bytes 5242880 | tf_op jit(solution)/shard_map/reduce_scatter | solution.py:203
  1058.6 69.3 %copy-start.4 = (bf16[512,1024]{1,0:T(8,128)(2,1)S(1)}, bf16[512,1024]{1,0:T(8,128)(2,1)}, u32[]{:S(2)}) copy-start(bf16[512,1024]{1,0:T(8,128)(2,1)} %param.22) | copy-start | bytes 3145732
  1058.6 69.3 %copy-start.29 = (f32[1024]{0:T(1024)S(1)}, f32[1024]{0:T(1024)}, u32[]{:S(2)}) copy-start(f32[1024]{0:T(1024)} %copy-done.28) | copy-start | bytes 12292
  1058.6 69.3 %copy-start.31 = (f32[512]{0:T(512)S(1)}, f32[512]{0:T(512)}, u32[]{:S(2)}) copy-start(f32[512]{0:T(512)} %copy-done.30) | copy-start | bytes 6148
  1058.6 69.3 %copy-start.33 = (f32[512]{0:T(512)S(1)}, f32[512]{0:T(512)}, u32[]{:S(2)}) copy-start(f32[512]{0:T(512)} %copy-done.32) | copy-start | bytes 6148
  1058.7 71.5 %copy-start.34 = (f32[1024]{0:T(1024)S(1)}, f32[1024]{0:T(1024)}, u32[]{:S(2)}) copy-start(f32[1024]{0:T(1024)} %get-tuple-element.198) | copy-start | bytes 12292
  1058.7 71.5 %copy-start.35 = (f32[1024]{0:T(1024)S(1)}, f32[1024]{0:T(1024)}, u32[]{:S(2)}) copy-start(f32[1024]{0:T(1024)} %get-tuple-element.204) | copy-start | bytes 12292
  1058.7 71.5 %copy-start.36 = (f32[1024]{0:T(1024)S(1)}, f32[1024]{0:T(1024)}, u32[]{:S(2)}) copy-start(f32[1024]{0:T(1024)} %get-tuple-element.261) | copy-start | bytes 12292
  1058.7 71.5 %copy-start.37 = (f32[1024]{0:T(1024)S(1)}, f32[1024]{0:T(1024)}, u32[]{:S(2)}) copy-start(f32[1024]{0:T(1024)} %get-tuple-element.268) | copy-start | bytes 12292
  1058.7 116.8 %copy-start.1 = (bf16[1024,1024]{1,0:T(8,128)(2,1)S(1)}, bf16[1024,1024]{1,0:T(8,128)(2,1)}, u32[]{:S(2)}) copy-start(bf16[1024,1024]{1,0:T(8,128)(2,1)} %param.35) | copy-start | bytes 6291460
  (56 other events, 293.3 us)
Sparse Core Ops, SparseCore 0:
  14.7 83.4 all-gather.3
  186.3 75.2 reduce-scatter.4
  266.9 81.2 all-gather.5
  349.6 79.2 all-gather.7
  449.1 75.2 reduce-scatter.8
  526.6 77.2 reduce-scatter.6
  944.1 104.4 all-reduce.4
  1050.9 76.9 reduce-scatter.10
